TPU v7x, 256 devices: a whole 4x4x8 slice. The times are simulated.
256 devices in a mesh: row: 32 (over x, y, core), col: 8 (over z).
Axes of the slice: x: 4, y: 4, z: 8, core: 2. Of those that a mesh axis runs over, the one named last changes fastest.
Arguments:
- object_field: float32 [2, 24576, 4096], P(None, 'row', 'col'), may hold values from -6 to 6
- probe: float32 [2, 256, 256], replicated, may hold values from -6 to 6
- amplitudes: bfloat16 [32, 8, 3, 4, 256, 256], P('row', 'col'), may hold values from 0 to 2
- positions: int32 [32, 8, 3, 4, 2], P('row', 'col'), may hold values from -128 to 640, as said below
- counts: int32 [32, 8, 3], P('row', 'col'), may hold values from 1 to 4, as said below
Outputs:
- gradient: float32 [2, 24576, 4096], P(None, 'row', 'col')
- updated_object: float32 [2, 24576, 4096], P(None, 'row', 'col')
Inputs may be any that keep to these rules, and one draw needn't show every extreme that they name: `positions`: offsets lie from -128 to 640 for rows and from -128 to 384 for columns. In every tile slot 0 of micro-batch 0 sits at row -128 and column 384, and slot 0 of micro-batch 1 at row 640 and column -128. `counts`: slots 0 to count - 1 are live. Some tile has 4 live slots in every micro-batch.
All inputs are finite; a program needn't handle non-finite values.
Results may differ from a plain program's by a relative error of at most 0.0059.
Values may be sent and summed in bfloat16 or wider, within the bound.
No kernel may reach another device: no remote copies, remote signals or barrier semaphores. Data moves between devices by JAX's collectives and lax.ppermute only.
A program may use at most 128 MiB of HBM per device.

v0:
```python
import functools
import math

import jax
import jax.numpy as jnp
import ml_dtypes
import numpy as np
from jax import lax
from jax.experimental import pallas as pl
from jax.experimental.pallas import tpu as pltpu
from jax.sharding import PartitionSpec as P

step_scale = 0.5
LANES = 128
PACK = 16
CHUNK = 32
GROUP = 2
f32 = jnp.float32
bf16 = jnp.bfloat16
VMEM = pl.BlockSpec(memory_space=pltpu.VMEM)
SMEM = pl.BlockSpec(memory_space=pltpu.SMEM)
ANY = pl.BlockSpec(memory_space=pl.ANY)


def swap(block, axis, parity):
    size = lax.axis_size(axis)
    route = []
    for i in range(parity, size - 1, 2):
        route += [(i, i + 1), (i + 1, i)]
    return lax.ppermute(block, axis, route)


def even(axis):
    return lax.rem(lax.axis_index(axis), 2) == 0


def dft_parts(window):
    counter = np.arange(window)
    angles = 2.0 * math.pi / window * (counter[:, None] * counter[None, :] % window)
    scale_value = 1.0 / math.sqrt(window)
    parts = np.stack([np.cos(angles), -np.sin(angles)]) * scale_value
    return parts.astype(np.float32).astype(ml_dtypes.bfloat16)


def meta_rows(pos_ref, counts_ref):
    batches, slots = pos_ref.shape[2], pos_ref.shape[4]
    lane = lax.broadcasted_iota(jnp.int32, (PACK, LANES), 1)
    row = jnp.zeros((PACK, LANES), jnp.int32)
    fields = 2 * batches * slots
    for k in range(fields):
        value = pos_ref[0, 0, k // (2 * slots), k % 2, k // 2 % slots] + LANES
        row = jnp.where(lane == k, value // 16, row)
        row = jnp.where(lane == fields + k, lax.rem(value, 16), row)
    for k in range(batches):
        row = jnp.where(lane == 2 * fields + k, counts_ref[0, 0, k], row)
    return row.astype(f32).astype(bf16)


def edges_kernel(pos_ref, counts_ref, obj_hbm, first_ref, second_ref, low, high, sem):
    tile_r, tile_c = obj_hbm.shape[1:]
    part = 256
    copies = []
    for k in range(2 * tile_r // part):
        c, r = divmod(k * part, tile_r)
        for side, (start, target) in enumerate(((0, low), (tile_c - LANES, high))):
            source = obj_hbm.at[c, pl.ds(r, part), pl.ds(start, LANES)]
            copies.append(pltpu.make_async_copy(source, target.at[pl.ds(k * part, part), :], sem.at[side, k]))
    for copy in copies:
        copy.start()
    upward = even("col")
    meta = meta_rows(pos_ref, counts_ref)
    first_ref[2 * tile_r :, :] = meta
    second_ref[2 * tile_r :, :] = meta
    for k in range(2 * tile_r // part):
        copies[2 * k].wait()
        copies[2 * k + 1].wait()
        rows = slice(k * part, (k + 1) * part)
        a, b = low[rows, :], high[rows, :]
        first_ref[rows, :] = jnp.where(upward, b, a).astype(bf16)
        second_ref[rows, :] = jnp.where(upward, a, b).astype(bf16)


def prepare_kernel(obj_hbm, obj_ref, pa_ref, pb_ref, sem):
    tile_r, tile_c = obj_hbm.shape[1:]
    margin = (obj_ref.shape[2] - tile_r) // 2
    tiles = tile_c // LANES
    body = pl.ds(margin, tile_r)
    copies = [
        pltpu.make_async_copy(
            obj_hbm.at[c, :, pl.ds(LANES * t, LANES)], obj_ref.at[c, t + 1, body, :], sem.at[c, t]
        )
        for c in range(2)
        for t in range(tiles)
    ]
    for copy in copies:
        copy.start()
    downward = even("row")
    for k, copy in enumerate(copies):
        copy.wait()
        c, t = divmod(k, tiles)
        obj_ref[c, t + 1, body, :] = obj_ref[c, t + 1, body, :].astype(bf16).astype(f32)
        top = obj_ref[c, t + 1, margin : 2 * margin, :]
        bottom = obj_ref[c, t + 1, tile_r : tile_r + margin, :]
        rows = slice(k * margin, (k + 1) * margin)
        pa_ref[rows, :] = jnp.where(downward, bottom, top).astype(bf16)
        pb_ref[rows, :] = jnp.where(downward, top, bottom).astype(bf16)


def tables_kernel(base_ref, canvas_ref, fwd_ref, bwd_ref, ext_ref):
    win = base_ref.shape[1]
    canvas_ref[...] = jnp.zeros_like(canvas_ref)
    real, imag = base_ref[0], base_ref[1]
    fwd_ref[:win, :win] = real
    fwd_ref[:win, win:] = -imag
    fwd_ref[win:, :win] = imag
    fwd_ref[win:, win:] = real
    bwd_ref[:win, :win] = real
    bwd_ref[:win, win:] = imag
    bwd_ref[win:, :win] = -imag
    bwd_ref[win:, win:] = real
    for n in range(2):
        for h in range(2):
            half = base_ref[n, :, LANES * h : LANES * (h + 1)].astype(f32)
            ext_ref[n, h, :win, :] = half
            ext_ref[n, h, win:, :] = half


def sides_kernel(pos_ref, counts_ref, obj_in, za_ref, zb_ref, obj_ref, ca_ref, cb_ref, meta_ref):
    tiles = obj_ref.shape[1] - 2
    margin = LANES
    tile_r = obj_ref.shape[2] - 2 * margin
    right_first = even("col")
    downward = even("row")
    for c in range(2):
        for r in range(0, tile_r, 128):
            rows = slice(c * tile_r + r, c * tile_r + r + 128)
            a = za_ref[rows, :].astype(f32)
            b = zb_ref[rows, :].astype(f32)
            at = slice(margin + r, margin + r + 128)
            obj_ref[c, 0, at, :] = jnp.where(right_first, b, a)
            obj_ref[c, tiles + 1, at, :] = jnp.where(right_first, a, b)
        for h, t in enumerate((0, tiles + 1)):
            top = obj_ref[c, t, margin : 2 * margin, :]
            bottom = obj_ref[c, t, tile_r : tile_r + margin, :]
            k = (2 * c + h) * margin
            ca_ref[k : k + margin, :] = jnp.where(downward, bottom, top).astype(bf16)
            cb_ref[k : k + margin, :] = jnp.where(downward, top, bottom).astype(bf16)
    tail = 4 * margin
    a = za_ref[2 * tile_r :, :].astype(f32)
    b = zb_ref[2 * tile_r :, :].astype(f32)
    own = meta_rows(pos_ref, counts_ref)
    metas = (jnp.where(right_first, b, a).astype(bf16), own, jnp.where(right_first, a, b).astype(bf16))
    for k, meta in enumerate(metas):
        rows = slice(tail + PACK * k, tail + PACK * (k + 1))
        ca_ref[rows, :] = meta
        cb_ref[rows, :] = meta
        meta_ref[PACK * k : PACK * (k + 1), :] = meta


def slots_kernel(kind, *refs):
    if kind in ("far", "near"):
        (pos_ref, counts_ref, obj_in, canvas_in, halo_ref, corner_ref, probe_ref, amp_ref, fwd_ref, bwd_ref, ext_ref,
         obj, canvas_ref, rim_ref, todo, prb, xs, hs, er) = refs
    else:
        (pos_ref, counts_ref, obj, canvas_in, probe_ref, amp_ref, fwd_ref, bwd_ref, ext_ref,
         canvas_ref, todo, prb, xs, hs, er) = refs
    batches, slots = pos_ref.shape[2], pos_ref.shape[4]
    win = probe_ref.shape[1]
    margin = win // 2
    tiles = obj.shape[1] - 2
    tile_r = obj.shape[2] - 2 * margin
    tile_c = tiles * LANES
    upper = even("row") == (kind == "far")
    place = pl.multiple_of(jnp.where(upper, 0, margin + tile_r), margin)
    if kind in ("far", "near"):
        for c in range(2):
            for t in range(tiles):
                k = (c * tiles + t) * margin
                obj[c, t + 1, pl.ds(place, margin), :] = halo_ref[k : k + margin, :].astype(f32)
            for h, t in enumerate((0, tiles + 1)):
                k = (2 * c + h) * margin
                obj[c, t, pl.ds(place, margin), :] = corner_ref[k : k + margin, :].astype(f32)

    def member(row, col):
        inside = (row >= 0) & (row <= tile_r - win)
        between = (col >= 0) & (col <= tile_c - win)
        if kind == "core":
            return inside & between
        if kind == "inner":
            return inside & jnp.logical_not(between)
        return jnp.logical_not(inside) & ((row < 0) == upper)

    def collect(slot, count):
        batch = slot // slots
        row = pos_ref[0, 0, batch, 0, slot - batch * slots]
        col = pos_ref[0, 0, batch, 1, slot - batch * slots]
        live = (slot - batch * slots < counts_ref[0, 0, batch]) & member(row, col)

        @pl.when(live)
        def _():
            todo[count] = slot

        return count + live.astype(jnp.int32)

    total = lax.fori_loop(0, batches * slots, collect, jnp.int32(0))
    lane = lax.broadcasted_iota(jnp.int32, (CHUNK, LANES), 1)

    def group(first, width):
        chosen = []
        for g in range(width):
            slot = todo[first + g]
            batch = slot // slots
            row = pos_ref[0, 0, batch, 0, slot - batch * slots] + margin
            col = pos_ref[0, 0, batch, 1, slot - batch * slots] + margin
            tile = col // LANES
            shift = col - tile * LANES
            chosen.append((slot, row, tile, jnp.minimum(tile + 2, tiles + 1), shift))

        def exit_waves(g):
            slot, row, tile, wrapped, shift = chosen[g]
            low = lane < shift
            for i in range(0, win, CHUNK):
                turned = []
                window = []
                for c in range(2):
                    one = pltpu.roll(probe_ref[c, i : i + CHUNK, 0:LANES], shift, 1)
                    two = pltpu.roll(probe_ref[c, i : i + CHUNK, LANES:], shift, 1)
                    turned.append((jnp.where(low, two, one), jnp.where(low, one, two)))
                    at = pl.ds(row + i, CHUNK)
                    window.append(
                        (jnp.where(low, obj[c, wrapped, at, :], obj[c, tile, at, :]), obj[c, tile + 1, at, :])
                    )
                for h in range(2):
                    pr, pi = turned[0][h], turned[1][h]
                    wr, wi = window[0][h], window[1][h]
                    prb[g, 0, h, i : i + CHUNK, :] = pr
                    prb[g, 1, h, i : i + CHUNK, :] = pi
                    cols = slice(win * g + LANES * h, win * g + LANES * (h + 1))
                    xs[i : i + CHUNK, cols] = (pr * wr - pi * wi).astype(bf16)
                    xs[win + i : win + i + CHUNK, cols] = (pr * wi + pi * wr).astype(bf16)

        def rolled_table(g):
            shift = chosen[g][4]
            for i in range(0, win, CHUNK):
                for h in range(2):
                    real = ext_ref[0, h, pl.ds(win - shift + i, CHUNK), :].astype(bf16)
                    imag = ext_ref[1, h, pl.ds(win - shift + i, CHUNK), :].astype(bf16)
                    a = slice(LANES * h, LANES * (h + 1))
                    b = slice(win + LANES * h, win + LANES * (h + 1))
                    er[g, i : i + CHUNK, a] = real
                    er[g, i : i + CHUNK, b] = imag
                    er[g, win + i : win + i + CHUNK, a] = -imag
                    er[g, win + i : win + i + CHUNK, b] = real

        def rows_dft(table_ref):
            for g in range(width):
                for part in range(2):
                    out = jnp.dot(
                        table_ref[win * part : win * (part + 1), :],
                        xs[:, win * g : win * (g + 1)],
                        preferred_element_type=f32,
                    )
                    hs[g, :, win * part : win * (part + 1)] = out.astype(bf16)

        def residual_waves(g):
            far = jnp.dot(hs[g], er[g], preferred_element_type=f32)
            real, imag = far[:, :win], far[:, win:]
            scale = 1.0 - amp_ref[chosen[g][0]].astype(f32) * lax.rsqrt(real * real + imag * imag + 1.0)
            xs[:win, win * g : win * (g + 1)] = (real * scale).astype(bf16)
            xs[win:, win * g : win * (g + 1)] = (imag * scale).astype(bf16)

        def accumulate(g):
            slot, row, tile, wrapped, shift = chosen[g]
            back = lax.dot_general(hs[g], er[g], (((1,), (1,)), ((), ())), preferred_element_type=f32)
            keep = lax.broadcasted_iota(jnp.int32, (win, LANES), 1) < shift
            at = pl.ds(row, win)
            for h in range(2):
                pr, pi = prb[g, 0, h], prb[g, 1, h]
                br = back[:, LANES * h : LANES * (h + 1)]
                bi = back[:, win + LANES * h : win + LANES * (h + 1)]
                terms = [pr * br + pi * bi, pr * bi - pi * br]
                for c in range(2):
                    if h == 0:
                        canvas_ref[c, tile, at, :] += jnp.where(keep, 0.0, terms[c])
                        canvas_ref[c, wrapped, at, :] += jnp.where(keep, terms[c], 0.0)
                    else:
                        canvas_ref[c, tile + 1, at, :] += terms[c]

        for g in range(width):
            exit_waves(g)
        rows_dft(fwd_ref)
        for g in range(width):
            rolled_table(g)
        for g in range(width):
            residual_waves(g)
        rows_dft(bwd_ref)
        for g in range(width):
            accumulate(g)

    def full_group(p, carry):
        group(p * GROUP, GROUP)
        return carry

    lax.fori_loop(0, total // GROUP, full_group, 0)

    @pl.when(lax.rem(total, GROUP) == 1)
    def _():
        group(total - 1, 1)

    if kind in ("far", "near"):
        for c in range(2):
            for t in range(tiles + 2):
                k = (c * (tiles + 2) + t) * margin
                rim_ref[k : k + margin, :] = canvas_ref[c, t, pl.ds(place, margin), :].astype(bf16)
        spare = 2 * (tiles + 2) * margin
        if rim_ref.shape[0] > spare:
            rim_ref[spare:, :] = jnp.zeros((rim_ref.shape[0] - spare, LANES), bf16)


def light_kernel(meta_ref, ya_ref, yb_ref, probe_ref, scale_ref, power, light, rows_ref, table_ref, sem):
    win = probe_ref.shape[1]
    tiles, tile_r = scale_ref.shape[:2]
    tile_c = tiles * LANES
    batches = 3
    slots = 4
    step = 2 * batches * slots
    lower_first = even("row")
    tail = ya_ref.shape[0] - 3 * PACK
    for k in range(3):
        rows = slice(tail + PACK * k, tail + PACK * (k + 1))
        a, b = ya_ref[rows, :].astype(f32), yb_ref[rows, :].astype(f32)
        rows_ref[k : k + 1, :] = jnp.where(lower_first, b, a)[0:1].astype(jnp.int32)
        rows_ref[3 + k : 4 + k, :] = meta_ref[PACK * k : PACK * (k + 1), :].astype(f32)[0:1].astype(jnp.int32)
        rows_ref[6 + k : 7 + k, :] = jnp.where(lower_first, a, b)[0:1].astype(jnp.int32)
    copy = pltpu.make_async_copy(rows_ref, table_ref, sem)
    copy.start()
    for t in range(tiles + 4):
        light[t] = jnp.zeros_like(light[t])
    for h in range(2):
        cols = slice(LANES * h, LANES * (h + 1))
        real, imag = probe_ref[0, :, cols], probe_ref[1, :, cols]
        power[h] = real * real + imag * imag
    copy.wait()

    def tile_slots(n, carry):
        down = n // 3 - 1
        across = n - (down + 1) * 3 - 1

        def one(slot, inner):
            row = table_ref[n, 2 * slot] * 16 + table_ref[n, step + 2 * slot] - LANES + down * tile_r
            col = table_ref[n, 2 * slot + 1] * 16 + table_ref[n, step + 2 * slot + 1] - LANES + across * tile_c
            meets = (row > -win) & (row < tile_r) & (col > -win) & (col < tile_c)

            @pl.when(meets)
            def _():
                place = col + win
                tile = place // LANES
                shift = place - tile * LANES
                low = lax.broadcasted_iota(jnp.int32, (64, LANES), 1) < shift
                for i in range(0, win, 64):
                    one_half = pltpu.roll(power[0, i : i + 64, :], shift, 1)
                    two_half = pltpu.roll(power[1, i : i + 64, :], shift, 1)
                    at = pl.ds(row + win + i, 64)
                    light[tile, at, :] += jnp.where(low, 0.0, one_half)
                    light[tile + 1, at, :] += jnp.where(low, one_half, two_half)
                    light[tile + 2, at, :] += jnp.where(low, two_half, 0.0)

            return inner

        for batch in range(batches):
            carry = lax.fori_loop(slots * batch, slots * batch + table_ref[n, 2 * step + batch], one, carry)
        return carry

    lax.fori_loop(0, 9, tile_slots, 0)
    for t in range(tiles):
        scale_ref[t] = step_scale / (light[t + 2, win : win + tile_r, :] + 1.0)


def strips_kernel(canvas_ref, ya_ref, yb_ref, sa_ref, sb_ref):
    tiles = canvas_ref.shape[1] - 2
    margin = LANES
    tile_r = canvas_ref.shape[2] - 2 * margin
    lower_first = even("row")
    right_first = even("col")
    for c in range(2):
        for r in range(0, tile_r, margin):
            sides = []
            for t in (0, tiles + 1):
                value = canvas_ref[c, t, margin + r : 2 * margin + r, :]
                k = (c * (tiles + 2) + t) * margin
                a, b = ya_ref[k : k + margin, :].astype(f32), yb_ref[k : k + margin, :].astype(f32)
                if r == 0:
                    value += jnp.where(lower_first, b, a)
                if r == tile_r - margin:
                    value += jnp.where(lower_first, a, b)
                sides.append(value)
            rows = slice(c * tile_r + r, c * tile_r + r + margin)
            sa_ref[rows, :] = jnp.where(right_first, sides[1], sides[0]).astype(bf16)
            sb_ref[rows, :] = jnp.where(right_first, sides[0], sides[1]).astype(bf16)


def update_kernel(parity, *refs):
    outer = parity is not None
    if outer:
        obj_ref, canvas_ref, ya_ref, yb_ref, scale_ref, side_ref, _, _, grad_hbm, out_hbm, grad, out, sem = refs
    else:
        obj_ref, canvas_ref, ya_ref, yb_ref, scale_ref, grad_hbm, out_hbm, grad, out, sem = refs
    tiles = canvas_ref.shape[1] - 2
    margin = LANES
    tile_r = canvas_ref.shape[2] - 2 * margin
    part = 256
    lower_first = even("row")
    rightmost = jnp.where(even("col") == (parity == 0), tiles - 1, 0)
    copies = []
    for r in range(0, tile_r, part):
        for k, t in enumerate((rightmost,) if outer else range(1, tiles - 1)):
            cols = pl.ds(pl.multiple_of(LANES * t, LANES), LANES) if outer else pl.ds(LANES * t, LANES)
            rows = slice(r, r + part)
            for c in range(2):
                value = canvas_ref[c, t + 1, margin + r : margin + r + part, :]
                if outer:
                    value += side_ref[c * tile_r + r : c * tile_r + r + part, :].astype(f32)
                if r == 0 or r + part == tile_r:
                    at = (c * (tiles + 2) + t + 1) * margin
                    strip = pl.ds(pl.multiple_of(at, margin), margin) if outer else pl.ds(at, margin)
                    a = ya_ref[strip, :].astype(f32)
                    b = yb_ref[strip, :].astype(f32)
                    if r == 0:
                        top = value[:margin] + jnp.where(lower_first, b, a)
                        value = jnp.concatenate([top, value[margin:]], 0)
                    else:
                        bottom = value[part - margin :] + jnp.where(lower_first, a, b)
                        value = jnp.concatenate([value[: part - margin], bottom], 0)
                grad[c, k, rows, :] = value
                out[c, k, rows, :] = obj_ref[c, rows, cols] - scale_ref[t, rows, :] * value
            for n, (source, target) in enumerate(((grad, grad_hbm), (out, out_hbm))):
                copy = pltpu.make_async_copy(
                    source.at[:, k, pl.ds(r, part), :],
                    target.at[:, pl.ds(r, part), cols],
                    sem.at[n, k, r // part],
                )
                copy.start()
                copies.append(copy)
    for copy in copies:
        copy.wait()


def on_device(object_field, probe, amplitudes, positions, counts):
    tile_r, tile_c = object_field.shape[1:]
    window = probe.shape[1]
    margin = window // 2
    batches, slots = amplitudes.shape[2:4]
    tiles = tile_c // LANES
    padded = (2, tiles + 2, tile_r + 2 * margin, LANES)
    base = dft_parts(window)
    places = jnp.swapaxes(positions, 3, 4)
    shape = jax.ShapeDtypeStruct
    side = shape((2 * tile_r + PACK, LANES), bf16)
    strip = shape((2 * (tiles + 2) * margin, LANES), bf16)

    za, zb = pl.pallas_call(
        edges_kernel,
        out_shape=(side, side),
        in_specs=[SMEM, SMEM, ANY],
        out_specs=(VMEM, VMEM),
        scratch_shapes=[pltpu.VMEM((2 * tile_r, LANES), f32)] * 2 + [pltpu.SemaphoreType.DMA((2, 2 * tile_r // 256))],
        name="edges",
    )(places, counts, object_field)
    za, zb = swap(za, "col", 0), swap(zb, "col", 1)
    block = shape((2 * window, 2 * window), bf16)
    row_halo = shape((2 * tiles * margin, LANES), bf16)
    obj, pa, pb = pl.pallas_call(
        prepare_kernel,
        out_shape=(shape(padded, f32), row_halo, row_halo),
        in_specs=[ANY],
        out_specs=(VMEM,) * 3,
        scratch_shapes=[pltpu.SemaphoreType.DMA((2, tiles))],
        compiler_params=pltpu.CompilerParams(vmem_limit_bytes=4 << 20),
        cost_estimate=pl.CostEstimate(flops=4 << 20, bytes_accessed=16 << 20, transcendentals=0),
        name="prepare",
    )(object_field)
    pb, pa = swap(pb, "row", 1), swap(pa, "row", 0)
    obj, base = lax.optimization_barrier((obj, jnp.asarray(base)))
    canvas, fwd, bwd, ext = pl.pallas_call(
        tables_kernel,
        out_shape=(shape(padded, f32), block, block, shape((2, 2, 2 * window, LANES), f32)),
        in_specs=[VMEM],
        out_specs=(VMEM,) * 4,
        compiler_params=pltpu.CompilerParams(vmem_limit_bytes=4 << 20),
        cost_estimate=pl.CostEstimate(flops=4 << 20, bytes_accessed=8 << 20, transcendentals=0),
        name="tables",
    )(base)
    obj, canvas, fwd, bwd, ext = lax.optimization_barrier((obj, canvas, fwd, bwd, ext))
    amps = amplitudes.reshape(batches * slots, window, window)
    tail = (probe, amps, fwd, bwd, ext)

    long_strip = shape((strip.shape[0] + margin, LANES), bf16)

    def run(kind, obj, canvas, *halo):
        edge = bool(halo)
        big = shape(padded, f32)
        return pl.pallas_call(
            functools.partial(slots_kernel, kind),
            out_shape=(big, big, long_strip if kind == "far" else strip) if edge else big,
            in_specs=[SMEM, SMEM] + [VMEM] * (7 + len(halo)),
            out_specs=(VMEM,) * 3 if edge else VMEM,
            input_output_aliases={2: 0, 3: 1} if edge else {3: 0},
            scratch_shapes=[
                pltpu.SMEM((batches * slots,), jnp.int32),
                pltpu.VMEM((GROUP, 2, 2, window, LANES), f32),
                pltpu.VMEM((2 * window, GROUP * window), bf16),
                pltpu.VMEM((GROUP, window, 2 * window), bf16),
                pltpu.VMEM((GROUP, 2 * window, 2 * window), bf16),
            ],
            compiler_params=pltpu.CompilerParams(vmem_limit_bytes=14 << 20),
            cost_estimate=pl.CostEstimate(flops=2 << 30, bytes_accessed=8 << 20, transcendentals=0),
            name=kind,
        )(places, counts, obj, canvas, *halo, *tail)

    packed = shape((4 * margin + 3 * PACK, LANES), bf16)
    obj, ca, cb, meta = pl.pallas_call(
        sides_kernel,
        out_shape=(shape(padded, f32), packed, packed, shape((3 * PACK, LANES), bf16)),
        in_specs=[SMEM, SMEM] + [VMEM] * 3,
        out_specs=(VMEM,) * 4,
        input_output_aliases={2: 0},
        compiler_params=pltpu.CompilerParams(vmem_limit_bytes=4 << 20),
        name="sides",
    )(places, counts, obj, za, zb)
    cb, ca = swap(cb, "row", 1), swap(ca, "row", 0)
    canvas = run("inner", obj, canvas)
    obj, canvas, rb = run("far", obj, canvas, pb, cb)
    rb = swap(rb, "row", 1)
    obj, canvas, ra = run("near", obj, canvas, pa, ca)
    ra = swap(ra, "row", 0)
    canvas = run("core", obj, canvas)
    rim = shape((2 * tile_r, LANES), bf16)
    sa, sb = pl.pallas_call(
        strips_kernel,
        out_shape=(rim, rim),
        in_specs=[VMEM] * 3,
        out_specs=(VMEM, VMEM),
        compiler_params=pltpu.CompilerParams(vmem_limit_bytes=4 << 20),
        name="strips",
    )(canvas, ra, rb)
    sa, sb, probe = lax.optimization_barrier((sa, sb, probe))
    sa, sb = swap(sa, "col", 0), swap(sb, "col", 1)
    scale = pl.pallas_call(
        light_kernel,
        out_shape=shape((tiles, tile_r, LANES), f32),
        in_specs=[VMEM] * 4,
        out_specs=VMEM,
        scratch_shapes=[
            pltpu.VMEM((2, window, LANES), f32),
            pltpu.VMEM((tiles + 4, tile_r + 2 * window, LANES), f32),
            pltpu.VMEM((PACK, LANES), jnp.int32),
            pltpu.SMEM((PACK, LANES), jnp.int32),
            pltpu.SemaphoreType.DMA,
        ],
        compiler_params=pltpu.CompilerParams(vmem_limit_bytes=9 << 20),
        cost_estimate=pl.CostEstimate(flops=8 << 20, bytes_accessed=12 << 20, transcendentals=0),
        name="light",
    )(meta, ca, cb, probe)
    field = shape((2, tile_r, tile_c), f32)

    def update(parity, aliases, *args):
        width = 2 if parity is None else 1
        return pl.pallas_call(
            functools.partial(update_kernel, parity),
            out_shape=(field, field),
            in_specs=[VMEM] * (len(args) - len(aliases)) + [ANY] * len(aliases),
            out_specs=(ANY, ANY),
            input_output_aliases=aliases,
            scratch_shapes=[pltpu.VMEM((2, width, tile_r, LANES), f32)] * 2
            + [pltpu.SemaphoreType.DMA((2, width, tile_r // 256))],
            compiler_params=pltpu.CompilerParams(vmem_limit_bytes=8 << 20),
            cost_estimate=pl.CostEstimate(flops=4 << 20, bytes_accessed=10 << 20, transcendentals=0),
            name="middle" if parity is None else "rim",
        )(*args)

    grad, out = update(None, {}, object_field, canvas, ra, rb, scale)
    grad, out = update(0, {6: 0, 7: 1}, object_field, canvas, ra, rb, scale, sa, grad, out)
    return update(1, {6: 0, 7: 1}, object_field, canvas, ra, rb, scale, sb, grad, out)


def solution(mesh):
    in_specs = (
        P(None, "row", "col"),
        P(),
        P("row", "col", None, None, None, None),
        P("row", "col", None, None, None),
        P("row", "col", None),
    )
    out_specs = (P(None, "row", "col"), P(None, "row", "col"))
    return jax.shard_map(
        on_device, mesh=mesh, in_specs=in_specs, out_specs=out_specs, check_vma=False
    )
```

profile of v0, /device:TPU:102, one launch (start us, length us, event | category | flops | bytes accessed | tf_op | source)
XLA Modules:
  0.0 58.9 jit_solution(14496902293266747901)
XLA Ops:
  0.6 0.0 copy-start.4
  0.7 3.3 %edges.1 = (bf16[1552,128]{1,0:T(8,128)(2,1)}, bf16[1552,128]{1,0:T(8,128)(2,1)}) custom-call(s32[1,1,3,2,4]{4,3,2,1,0:T(2,128)} %bitcast.6, s32[1,1,3]{2,1,0:T(1,128)} %refs_1_.7, f32[2,768,512]{2,1,0:T(8,128)} %refs_0_.5), custom_call_target="tpu_custom_call" | custom-call | tf_op jit(solution)/shard_map/edges/pallas_call | solution.py:461
  4.0 0.2 collective-permute-start
  4.2 5.9 %collective-permute-start.1 = (bf16[1552,128]{1,0:T(8,128)(2,1)}, bf16[1552,128]{1,0:T(8,128)(2,1)S(1)}, u32[]{:S(2)}, u32[]{:S(2)}) collective-permute-start(bf16[1552,128]{1,0:T(8,128)(2,1)} %get-tuple-element.46), channel_id=1, source_target_pairs={{1,2},{2,1},{3,4},{4,3},{5,6},{6,5},{9,10},{10,9},{11,12},{12,11},... | collective-permute-start | bytes 1191944 | tf_op jit(solution)/shard_map/ppermute | solution.py:30
  10.1 0.0 copy-start
  10.1 1.9 %copy-done = f32[2,768,512]{2,1,0:T(8,128)S(1)} copy-done((f32[2,768,512]{2,1,0:T(8,128)S(1)}, f32[2,768,512]{2,1,0:T(8,128)}, u32[]{:S(2)}) %copy-start) | copy-done | bytes 3145752
  12.0 0.8 %prepare.1 = (f32[2,6,1024,128]{3,2,1,0:T(8,128)S(1)}, bf16[1024,128]{1,0:T(8,128)(2,1)S(1)}, bf16[1024,128]{1,0:T(8,128)(2,1)S(1)}) custom-call(f32[2,768,512]{2,1,0:T(8,128)S(1)} %copy-done), custom_call_target="tpu_custom_call" | custom-call | flops 4194304 | bytes 16777216 | tf_op jit(solution)/shard_map/prepare/pallas_call | solution.py:472
  12.8 4.1 %collective-permute-start.2 = (bf16[1024,128]{1,0:T(8,128)(2,1)S(1)}, bf16[1024,128]{1,0:T(8,128)(2,1)S(1)}, u32[]{:S(2)}, u32[]{:S(2)}) collective-permute-start(bf16[1024,128]{1,0:T(8,128)(2,1)S(1)} %get-tuple-element.52), channel_id=1, source_target_pairs={{8,16},{16,8},{24,32},{32,24},{40,48},{48,40},{56,64},{64,56},{72,... | collective-permute-start | bytes 786440 | tf_op jit(solution)/shard_map/ppermute | solution.py:30
  16.9 0.1 collective-permute-start.4
  17.0 0.5 tables.1
  17.6 1.7 %collective-permute-done.1.zb_ref = bf16[1552,128]{1,0:T(8,128)(2,1)S(1)} collective-permute-done((bf16[1552,128]{1,0:T(8,128)(2,1)}, bf16[1552,128]{1,0:T(8,128)(2,1)S(1)}, u32[]{:S(2)}, u32[]{:S(2)}) %collective-permute-start.1) | collective-permute-done | bytes 397344 | tf_op jit(solution)/shard_map/ppermute | solution.py:30
  19.3 0.8 %sides.1 = (f32[2,6,1024,128]{3,2,1,0:T(8,128)S(1)}, bf16[560,128]{1,0:T(8,128)(2,1)S(1)}, bf16[560,128]{1,0:T(8,128)(2,1)S(1)}, bf16[48,128]{1,0:T(8,128)(2,1)S(1)}) custom-call(s32[1,1,3,2,4]{4,3,2,1,0:T(2,128)S(1)} %bitcast.7, s32[1,1,3]{2,1,0:T(1,128)S(1)} %copy-done.6, ...), custom_call_target="tpu_custom_call", output_to_operand_aliasing={{0}: (2, {})} | custom-call | tf_op jit(solution)/shard_map/sides/pallas_call | solution.py:521
  20.1 3.8 %collective-permute-start.3 = (bf16[560,128]{1,0:T(8,128)(2,1)S(1)}, bf16[560,128]{1,0:T(8,128)(2,1)S(1)}, u32[]{:S(2)}, u32[]{:S(2)}) collective-permute-start(bf16[560,128]{1,0:T(8,128)(2,1)S(1)} %get-tuple-element.53), channel_id=1, source_target_pairs={{8,16},{16,8},{24,32},{32,24},{40,48},{48,40},{56,64},{64,56},{72,... | collective-permute-start | bytes 430088 | tf_op jit(solution)/shard_map/ppermute | solution.py:30
  23.8 0.1 collective-permute-start.5
  24.0 0.9 %inner.1.refs_3_ = f32[2,6,1024,128]{3,2,1,0:T(8,128)S(1)} custom-call(s32[1,1,3,2,4]{4,3,2,1,0:T(2,128)S(1)} %bitcast.8, s32[1,1,3]{2,1,0:T(1,128)S(1)} %copy-done.6, f32[2,6,1024,128]{3,2,1,0:T(8,128)S(1)} %get-tuple-element.47.refs_2_, f32[2,6,1024,128]{3,2,1,0:T(8,128)S(1)} %get-tuple-element.48.refs_3_, ...), custom_call_target="tpu_custom_call", output_to_operand_aliasing={{}: (3, {})} | custom-call | flops 2147483648 | bytes 8388608 | tf_op jit(solution)/shard_map/inner/pallas_call | solution.py:502
  24.8 3.8 %collective-permute-done.3.refs_5_.yb_ref = bf16[560,128]{1,0:T(8,128)(2,1)S(1)} collective-permute-done((bf16[560,128]{1,0:T(8,128)(2,1)S(1)}, bf16[560,128]{1,0:T(8,128)(2,1)S(1)}, u32[]{:S(2)}, u32[]{:S(2)}) %collective-permute-start.3) | collective-permute-done | bytes 143392 | tf_op jit(solution)/shard_map/ppermute | solution.py:30
  28.6 2.4 %far.1 = (f32[2,6,1024,128]{3,2,1,0:T(8,128)S(1)}, f32[2,6,1024,128]{3,2,1,0:T(8,128)S(1)}, bf16[1664,128]{1,0:T(8,128)(2,1)S(1)}) custom-call(s32[1,1,3,2,4]{4,3,2,1,0:T(2,128)S(1)} %bitcast.9, s32[1,1,3]{2,1,0:T(1,128)S(1)} %copy-done.6, f32[2,6,1024,128]{3,2,1,0:T(8,128)S(1)} %get-tuple-element.47.refs_2_, ...), custom_call_target="tpu_custom_call", output_to_operand_aliasing={{0}: (2, {}), {1}: (3, {})} | custom-call | flops 2147483648 | bytes 8388608 | tf_op jit(solution)/shard_map/far/pallas_call | solution.py:502
  31.0 4.1 %collective-permute-start.7 = (bf16[1664,128]{1,0:T(8,128)(2,1)S(1)}, bf16[1664,128]{1,0:T(8,128)(2,1)S(1)}, u32[]{:S(2)}, u32[]{:S(2)}) collective-permute-start(bf16[1664,128]{1,0:T(8,128)(2,1)S(1)} %get-tuple-element.61), channel_id=1, source_target_pairs={{8,16},{16,8},{24,32},{32,24},{40,48},{48,40},{56,64},{64,56},{72,... | collective-permute-start | bytes 1277960 | tf_op jit(solution)/shard_map/ppermute | solution.py:30
  35.0 0.0 collective-permute-done.4.refs_4_
  35.1 2.4 %near.1 = (f32[2,6,1024,128]{3,2,1,0:T(8,128)S(1)}, f32[2,6,1024,128]{3,2,1,0:T(8,128)S(1)}, bf16[1536,128]{1,0:T(8,128)(2,1)S(1)}) custom-call(s32[1,1,3,2,4]{4,3,2,1,0:T(2,128)S(1)} %bitcast.10, s32[1,1,3]{2,1,0:T(1,128)S(1)} %copy-done.6, f32[2,6,1024,128]{3,2,1,0:T(8,128)S(1)} %get-tuple-element.54.refs_2_, ...), custom_call_target="tpu_custom_call", output_to_operand_aliasing={{0}: (2, {}), {1}: (3, {})} | custom-call | flops 2147483648 | bytes 8388608 | tf_op jit(solution)/shard_map/near/pallas_call | solution.py:502
  37.4 0.3 collective-permute-start.6
  37.7 2.2 %core.1.canvas_ref.refs_1_ = f32[2,6,1024,128]{3,2,1,0:T(8,128)S(1)} custom-call(s32[1,1,3,2,4]{4,3,2,1,0:T(2,128)S(1)} %bitcast.11, s32[1,1,3]{2,1,0:T(1,128)S(1)} %copy-done.6, f32[2,6,1024,128]{3,2,1,0:T(8,128)S(1)} %get-tuple-element.58.refs_2_, f32[2,6,1024,128]{3,2,1,0:T(8,128)S(1)} %get-tuple-element.59.refs_3_, ...), custom_call_target="tpu_custom_call", output_to_operand_aliasing={{}: (3, {})} | custom-call | flops 2147483648 | bytes 8388608 | tf_op jit(solution)/shard_map/core/pallas_call | solution.py:502
  40.0 0.0 copy-start.1
  40.0 2.5 %collective-permute-done.7.yb_ref.refs_3_ = bf16[1664,128]{1,0:T(8,128)(2,1)S(1)} collective-permute-done((bf16[1664,128]{1,0:T(8,128)(2,1)S(1)}, bf16[1664,128]{1,0:T(8,128)(2,1)S(1)}, u32[]{:S(2)}, u32[]{:S(2)}) %collective-permute-start.7) | collective-permute-done | bytes 426016 | tf_op jit(solution)/shard_map/ppermute | solution.py:30
  42.5 0.2 strips.1
  42.7 0.1 collective-permute-start.9
  42.8 6.2 %collective-permute-start.8 = (bf16[1536,128]{1,0:T(8,128)(2,1)S(1)}, bf16[1536,128]{1,0:T(8,128)(2,1)S(1)}, u32[]{:S(2)}, u32[]{:S(2)}) collective-permute-start(bf16[1536,128]{1,0:T(8,128)(2,1)S(1)} %get-tuple-element.66), channel_id=1, source_target_pairs={{1,2},{2,1},{3,4},{4,3},{5,6},{6,5},{9,10},{10,9},{11,12},{12,11},... | collective-permute-start | bytes 1179656 | tf_op jit(solution)/shard_map/ppermute | solution.py:30
  49.0 4.6 %light.1.refs_4_ = f32[4,768,128]{2,1,0:T(8,128)S(1)} custom-call(bf16[48,128]{1,0:T(8,128)(2,1)S(1)} %get-tuple-element.62.meta_ref, bf16[560,128]{1,0:T(8,128)(2,1)S(1)} %collective-permute-done.5.refs_5_.ya_ref, bf16[560,128]{1,0:T(8,128)(2,1)S(1)} %collective-permute-done.3.refs_5_.yb_ref, f32[2,256,256]{2,1,0:T(8,128)S(1)} %copy-done.3), custom_call_target="tpu_custom_call" | custom-call | flops 8388608 | bytes 12582912 | tf_op jit(solution)/shard_map/light/pallas_call | solution.py:548
  53.6 1.8 %middle.1 = (f32[2,768,512]{2,1,0:T(8,128)}, f32[2,768,512]{2,1,0:T(8,128)}) custom-call(f32[2,768,512]{2,1,0:T(8,128)S(1)} %copy-done.1, f32[2,6,1024,128]{3,2,1,0:T(8,128)S(1)} %core.1.canvas_ref.refs_1_, bf16[1536,128]{1,0:T(8,128)(2,1)S(1)} %collective-permute-done.6.ya_ref.refs_2_, bf16[1664,128]{1,0:T(8,128)(2,1)S(1)} %collective-permute-done.7.yb_ref.refs_3_, ...), custom_call_target="tpu_custom_call" | custom-call | flops 4194304 | bytes 10485760 | tf_op jit(solution)/shard_map/middle/pallas_call | solution.py:568
  55.5 1.3 %rim.2 = (f32[2,768,512]{2,1,0:T(8,128)}, f32[2,768,512]{2,1,0:T(8,128)}) custom-call(f32[2,768,512]{2,1,0:T(8,128)S(1)} %copy-done.1, f32[2,6,1024,128]{3,2,1,0:T(8,128)S(1)} %core.1.canvas_ref.refs_1_, bf16[1536,128]{1,0:T(8,128)(2,1)S(1)} %collective-permute-done.6.ya_ref.refs_2_, ...), custom_call_target="tpu_custom_call", output_to_operand_aliasing={{0}: (6, {}), {1}: (7, {})} | custom-call | flops 4194304 | bytes 10485760 | tf_op jit(solution)/shard_map/rim/pallas_call | solution.py:568
  56.8 0.7 %collective-permute-done.8.refs_5_ = bf16[1536,128]{1,0:T(8,128)(2,1)S(1)} collective-permute-done((bf16[1536,128]{1,0:T(8,128)(2,1)S(1)}, bf16[1536,128]{1,0:T(8,128)(2,1)S(1)}, u32[]{:S(2)}, u32[]{:S(2)}) %collective-permute-start.8) | collective-permute-done | bytes 393248 | tf_op jit(solution)/shard_map/ppermute | solution.py:30
  57.5 1.3 %rim.3 = (f32[2,768,512]{2,1,0:T(8,128)}, f32[2,768,512]{2,1,0:T(8,128)}) custom-call(f32[2,768,512]{2,1,0:T(8,128)S(1)} %copy-done.1, f32[2,6,1024,128]{3,2,1,0:T(8,128)S(1)} %core.1.canvas_ref.refs_1_, bf16[1536,128]{1,0:T(8,128)(2,1)S(1)} %collective-permute-done.6.ya_ref.refs_2_, ...), custom_call_target="tpu_custom_call", output_to_operand_aliasing={{0}: (6, {}), {1}: (7, {})} | custom-call | flops 4194304 | bytes 10485760 | tf_op jit(solution)/shard_map/rim/pallas_call | solution.py:568
  (15 shorter events, 0.0 us)
Async XLA Ops:
  0.6 16.4 %copy-start.4 = (bf16[2,256,256]{2,1,0:T(8,128)(2,1)S(1)}, bf16[2,256,256]{2,1,0:T(8,128)(2,1)}, u32[]{:S(2)}) copy-start(bf16[2,256,256]{2,1,0:T(8,128)(2,1)} %constant.2.clone.base_ref) | copy-start | bytes 786436
  0.6 18.6 %copy-start.6 = (s32[1,1,3]{2,1,0:T(1,128)S(1)}, s32[1,1,3]{2,1,0:T(1,128)}, u32[]{:S(2)}) copy-start(s32[1,1,3]{2,1,0:T(1,128)} %refs_1_.7) | copy-start | bytes 40
  0.7 18.6 %copy-start.5 = (s32[1,1,3,4,2]{3,4,2,1,0:T(2,128)S(1)}, s32[1,1,3,4,2]{3,4,2,1,0:T(2,128)}, u32[]{:S(2)}) copy-start(s32[1,1,3,4,2]{3,4,2,1,0:T(2,128)} %param.9) | copy-start | bytes 292
  0.7 23.3 %copy-start.2 = (bf16[1,1,3,4,256,256]{5,4,3,2,1,0:T(8,128)(2,1)S(1)}, bf16[1,1,3,4,256,256]{5,4,3,2,1,0:T(8,128)(2,1)}, u32[]{:S(2)}) copy-start(bf16[1,1,3,4,256,256]{5,4,3,2,1,0:T(8,128)(2,1)} %param.8) | copy-start | bytes 4718596
  0.7 23.3 %copy-start.3 = (f32[2,256,256]{2,1,0:T(8,128)S(1)}, f32[2,256,256]{2,1,0:T(8,128)}, u32[]{:S(2)}) copy-start(f32[2,256,256]{2,1,0:T(8,128)} %probe_ref) | copy-start | bytes 1572868
  4.0 13.6 %collective-permute-start = (bf16[1552,128]{1,0:T(8,128)(2,1)}, bf16[1552,128]{1,0:T(8,128)(2,1)S(1)}, u32[]{:S(2)}, u32[]{:S(2)}) collective-permute-start(bf16[1552,128]{1,0:T(8,128)(2,1)} %get-tuple-element.45), channel_id=1, source_target_pairs={{0,1},{1,0},{2,3},{3,2},{4,5},{5,4},{6,7},{7,6},{8,9},{9,8},{10,11... | collective-permute-start | bytes 1191944 | tf_op jit(solution)/shard_map/ppermute | solution.py:30
  4.2 15.1 %collective-permute-start.1 = (bf16[1552,128]{1,0:T(8,128)(2,1)}, bf16[1552,128]{1,0:T(8,128)(2,1)S(1)}, u32[]{:S(2)}, u32[]{:S(2)}) collective-permute-start(bf16[1552,128]{1,0:T(8,128)(2,1)} %get-tuple-element.46), channel_id=1, source_target_pairs={{1,2},{2,1},{3,4},{4,3},{5,6},{6,5},{9,10},{10,9},{11,12},{12,11},... | collective-permute-start | bytes 1191944 | tf_op jit(solution)/shard_map/ppermute | solution.py:30
  10.1 1.9 %copy-start = (f32[2,768,512]{2,1,0:T(8,128)S(1)}, f32[2,768,512]{2,1,0:T(8,128)}, u32[]{:S(2)}) copy-start(f32[2,768,512]{2,1,0:T(8,128)} %refs_0_.5) | copy-start | bytes 9437188
  12.8 12.0 %collective-permute-start.2 = (bf16[1024,128]{1,0:T(8,128)(2,1)S(1)}, bf16[1024,128]{1,0:T(8,128)(2,1)S(1)}, u32[]{:S(2)}, u32[]{:S(2)}) collective-permute-start(bf16[1024,128]{1,0:T(8,128)(2,1)S(1)} %get-tuple-element.52), channel_id=1, source_target_pairs={{8,16},{16,8},{24,32},{32,24},{40,48},{48,40},{56,64},{64,56},{72,... | collective-permute-start | bytes 786440 | tf_op jit(solution)/shard_map/ppermute | solution.py:30
  16.9 18.1 %collective-permute-start.4 = (bf16[1024,128]{1,0:T(8,128)(2,1)S(1)}, bf16[1024,128]{1,0:T(8,128)(2,1)S(1)}, u32[]{:S(2)}, u32[]{:S(2)}) collective-permute-start(bf16[1024,128]{1,0:T(8,128)(2,1)S(1)} %get-tuple-element.56), channel_id=1, source_target_pairs={{0,8},{8,0},{16,24},{24,16},{32,40},{40,32},{48,56},{56,48},{64,72... | collective-permute-start | bytes 786440 | tf_op jit(solution)/shard_map/ppermute | solution.py:30
  20.1 8.5 %collective-permute-start.3 = (bf16[560,128]{1,0:T(8,128)(2,1)S(1)}, bf16[560,128]{1,0:T(8,128)(2,1)S(1)}, u32[]{:S(2)}, u32[]{:S(2)}) collective-permute-start(bf16[560,128]{1,0:T(8,128)(2,1)S(1)} %get-tuple-element.53), channel_id=1, source_target_pairs={{8,16},{16,8},{24,32},{32,24},{40,48},{48,40},{56,64},{64,56},{72,... | collective-permute-start | bytes 430088 | tf_op jit(solution)/shard_map/ppermute | solution.py:30
  23.8 11.2 %collective-permute-start.5 = (bf16[560,128]{1,0:T(8,128)(2,1)S(1)}, bf16[560,128]{1,0:T(8,128)(2,1)S(1)}, u32[]{:S(2)}, u32[]{:S(2)}) collective-permute-start(bf16[560,128]{1,0:T(8,128)(2,1)S(1)} %get-tuple-element.57), channel_id=1, source_target_pairs={{0,8},{8,0},{16,24},{24,16},{32,40},{40,32},{48,56},{56,48},{64,72... | collective-permute-start | bytes 430088 | tf_op jit(solution)/shard_map/ppermute | solution.py:30
  31.0 11.6 %collective-permute-start.7 = (bf16[1664,128]{1,0:T(8,128)(2,1)S(1)}, bf16[1664,128]{1,0:T(8,128)(2,1)S(1)}, u32[]{:S(2)}, u32[]{:S(2)}) collective-permute-start(bf16[1664,128]{1,0:T(8,128)(2,1)S(1)} %get-tuple-element.61), channel_id=1, source_target_pairs={{8,16},{16,8},{24,32},{32,24},{40,48},{48,40},{56,64},{64,56},{72,... | collective-permute-start | bytes 1277960 | tf_op jit(solution)/shard_map/ppermute | solution.py:30
  37.4 2.5 %collective-permute-start.6 = (bf16[1536,128]{1,0:T(8,128)(2,1)S(1)}, bf16[1536,128]{1,0:T(8,128)(2,1)S(1)}, u32[]{:S(2)}, u32[]{:S(2)}) collective-permute-start(bf16[1536,128]{1,0:T(8,128)(2,1)S(1)} %get-tuple-element.60), channel_id=1, source_target_pairs={{0,8},{8,0},{16,24},{24,16},{32,40},{40,32},{48,56},{56,48},{64,72... | collective-permute-start | bytes 1179656 | tf_op jit(solution)/shard_map/ppermute | solution.py:30
  40.0 13.6 %copy-start.1 = (f32[2,768,512]{2,1,0:T(8,128)S(1)}, f32[2,768,512]{2,1,0:T(8,128)}, u32[]{:S(2)}) copy-start(f32[2,768,512]{2,1,0:T(8,128)} %refs_0_.5) | copy-start | bytes 9437188
  42.7 12.8 %collective-permute-start.9 = (bf16[1536,128]{1,0:T(8,128)(2,1)S(1)}, bf16[1536,128]{1,0:T(8,128)(2,1)S(1)}, u32[]{:S(2)}, u32[]{:S(2)}) collective-permute-start(bf16[1536,128]{1,0:T(8,128)(2,1)S(1)} %get-tuple-element.67), channel_id=1, source_target_pairs={{0,1},{1,0},{2,3},{3,2},{4,5},{5,4},{6,7},{7,6},{8,9},{9,8},{10,11... | collective-permute-start | bytes 1179656 | tf_op jit(solution)/shard_map/ppermute | solution.py:30
  42.8 14.7 %collective-permute-start.8 = (bf16[1536,128]{1,0:T(8,128)(2,1)S(1)}, bf16[1536,128]{1,0:T(8,128)(2,1)S(1)}, u32[]{:S(2)}, u32[]{:S(2)}) collective-permute-start(bf16[1536,128]{1,0:T(8,128)(2,1)S(1)} %get-tuple-element.66), channel_id=1, source_target_pairs={{1,2},{2,1},{3,4},{4,3},{5,6},{6,5},{9,10},{10,9},{11,12},{12,11},... | collective-permute-start | bytes 1179656 | tf_op jit(solution)/shard_map/ppermute | solution.py:30
where the time goes:
time: 58.9 us
  starting transfers between devices  24.8 us (42%)
  Pallas kernels  22.4 us (38%)
  waiting for transfers between devices  8.75 us (15%)
  local copies, waits for them, and re-layouts  1.91 us (3%)
  between operations  1.09 us (2%)
    ppermute x10, starting transfers between devices, swap(): return lax.ppermute(block, axis, route)  24.8 us
    ppermute x10, waiting for transfers between devices, swap(): return lax.ppermute(block, axis, route)  8.75 us
    pallas_call x4, Pallas kernels, run(): pl.pallas_call(functools.partial(slots_kernel, kind), out_shape=(big, big...  7.85 us
    pallas_call x1, Pallas kernels, on_device(): pl.pallas_call(light_kernel, out_shape=shape((tiles, tile_r, LANES), f32)...  4.6 us
    pallas_call x3, Pallas kernels, update(): pl.pallas_call(functools.partial(update_kernel, parity), out_shape=(field...  4.38 us
    pallas_call x1, Pallas kernels, on_device(): pl.pallas_call(edges_kernel, out_shape=(side, side), in_specs=[SMEM, SMEM...  3.31 us
    unnamed x14, local copies, waits for them, and re-layouts  1.91 us
  transfers between devices with their start and end apart: 10, of which 4 were waited for; matrix products, arithmetic and copies ran while one was open for 0% of the time, Pallas kernels for 30%

commit v1 on v0

--- a/solution.py
+++ b/solution.py
@@ -490,7 +490,6 @@
         cost_estimate=pl.CostEstimate(flops=4 << 20, bytes_accessed=8 << 20, transcendentals=0),
         name="tables",
     )(base)
-    obj, canvas, fwd, bwd, ext = lax.optimization_barrier((obj, canvas, fwd, bwd, ext))
     amps = amplitudes.reshape(batches * slots, window, window)
     tail = (probe, amps, fwd, bwd, ext)
 
@@ -517,6 +516,8 @@
             name=kind,
         )(places, counts, obj, canvas, *halo, *tail)
 
+    canvas = run("core", obj, canvas)
+    obj, canvas, za, zb = lax.optimization_barrier((obj, canvas, za, zb))
     packed = shape((4 * margin + 3 * PACK, LANES), bf16)
     obj, ca, cb, meta = pl.pallas_call(
         sides_kernel,
@@ -533,18 +534,6 @@
     rb = swap(rb, "row", 1)
     obj, canvas, ra = run("near", obj, canvas, pa, ca)
     ra = swap(ra, "row", 0)
-    canvas = run("core", obj, canvas)
-    rim = shape((2 * tile_r, LANES), bf16)
-    sa, sb = pl.pallas_call(
-        strips_kernel,
-        out_shape=(rim, rim),
-        in_specs=[VMEM] * 3,
-        out_specs=(VMEM, VMEM),
-        compiler_params=pltpu.CompilerParams(vmem_limit_bytes=4 << 20),
-        name="strips",
-    )(canvas, ra, rb)
-    sa, sb, probe = lax.optimization_barrier((sa, sb, probe))
-    sa, sb = swap(sa, "col", 0), swap(sb, "col", 1)
     scale = pl.pallas_call(
         light_kernel,
         out_shape=shape((tiles, tile_r, LANES), f32),
@@ -561,6 +550,17 @@
         cost_estimate=pl.CostEstimate(flops=8 << 20, bytes_accessed=12 << 20, transcendentals=0),
         name="light",
     )(meta, ca, cb, probe)
+    canvas, scale = lax.optimization_barrier((canvas, scale))
+    rim = shape((2 * tile_r, LANES), bf16)
+    sa, sb = pl.pallas_call(
+        strips_kernel,
+        out_shape=(rim, rim),
+        in_specs=[VMEM] * 3,
+        out_specs=(VMEM, VMEM),
+        compiler_params=pltpu.CompilerParams(vmem_limit_bytes=4 << 20),
+        name="strips",
+    )(canvas, ra, rb)
+    sa, sb = swap(sa, "col", 0), swap(sb, "col", 1)
     field = shape((2, tile_r, tile_c), f32)
 
     def update(parity, aliases, *args):

time: 58.9 us -> 62.1 us (1.054)
  the two profiles are of different devices: /device:TPU:102 before, /device:TPU:36 now
where the time goes in v1:
time: 62.1 us; the launch traced here: 61.8 us
  Pallas kernels  27.2 us (44%)
  starting transfers between devices  22.7 us (37%)
  waiting for transfers between devices  8.89 us (14%)
  local copies, waits for them, and re-layouts  1.91 us (3%)
  between operations  1.11 us (2%)
    ppermute x10, starting transfers between devices, swap(): return lax.ppermute(block, axis, route)  22.7 us
    pallas_call x4, Pallas kernels, run(): pl.pallas_call(functools.partial(slots_kernel, kind), out_shape=(big, big...  12.1 us
    ppermute x10, waiting for transfers between devices, swap(): return lax.ppermute(block, axis, route)  8.89 us
    pallas_call x1, Pallas kernels, on_device(): pl.pallas_call(light_kernel, out_shape=shape((tiles, tile_r, LANES), f32)...  5.17 us
    pallas_call x3, Pallas kernels, update(): pl.pallas_call(functools.partial(update_kernel, parity), out_shape=(field...  4.37 us
    pallas_call x1, Pallas kernels, on_device(): pl.pallas_call(edges_kernel, out_shape=(side, side), in_specs=[SMEM, SMEM...  3.31 us
    unnamed x14, local copies, waits for them, and re-layouts  1.91 us
  transfers between devices with their start and end apart: 10, of which 3 were waited for; matrix products, arithmetic and copies ran while one was open for 0% of the time, Pallas kernels for 36%

profile of v1, /device:TPU:36, one launch (start us, length us, event | category | flops | bytes accessed | tf_op | source)
XLA Modules:
  0.0 61.8 jit_solution(13138488673788858555)
XLA Ops:
  0.6 0.0 copy-start.4
  0.7 3.3 %edges.1 = (bf16[1552,128]{1,0:T(8,128)(2,1)}, bf16[1552,128]{1,0:T(8,128)(2,1)}) custom-call(s32[1,1,3,2,4]{4,3,2,1,0:T(2,128)} %bitcast.6, s32[1,1,3]{2,1,0:T(1,128)} %refs_1_.7, f32[2,768,512]{2,1,0:T(8,128)} %refs_0_.5), custom_call_target="tpu_custom_call" | custom-call | tf_op jit(solution)/shard_map/edges/pallas_call | solution.py:461
  4.0 0.2 collective-permute-start
  4.2 5.6 %collective-permute-start.1 = (bf16[1552,128]{1,0:T(8,128)(2,1)}, bf16[1552,128]{1,0:T(8,128)(2,1)S(1)}, u32[]{:S(2)}, u32[]{:S(2)}) collective-permute-start(bf16[1552,128]{1,0:T(8,128)(2,1)} %get-tuple-element.42), channel_id=1, source_target_pairs={{1,2},{2,1},{3,4},{4,3},{5,6},{6,5},{9,10},{10,9},{11,12},{12,11},... | collective-permute-start | bytes 1191944 | tf_op jit(solution)/shard_map/ppermute | solution.py:30
  9.8 0.0 copy-start
  9.8 1.9 %copy-done = f32[2,768,512]{2,1,0:T(8,128)S(1)} copy-done((f32[2,768,512]{2,1,0:T(8,128)S(1)}, f32[2,768,512]{2,1,0:T(8,128)}, u32[]{:S(2)}) %copy-start) | copy-done | bytes 3145752
  11.7 0.8 %prepare.1 = (f32[2,6,1024,128]{3,2,1,0:T(8,128)S(1)}, bf16[1024,128]{1,0:T(8,128)(2,1)S(1)}, bf16[1024,128]{1,0:T(8,128)(2,1)S(1)}) custom-call(f32[2,768,512]{2,1,0:T(8,128)S(1)} %copy-done), custom_call_target="tpu_custom_call" | custom-call | flops 4194304 | bytes 16777216 | tf_op jit(solution)/shard_map/prepare/pallas_call | solution.py:472
  12.5 3.8 %collective-permute-start.2 = (bf16[1024,128]{1,0:T(8,128)(2,1)S(1)}, bf16[1024,128]{1,0:T(8,128)(2,1)S(1)}, u32[]{:S(2)}, u32[]{:S(2)}) collective-permute-start(bf16[1024,128]{1,0:T(8,128)(2,1)S(1)} %get-tuple-element.48), channel_id=1, source_target_pairs={{8,16},{16,8},{24,32},{32,24},{40,48},{48,40},{56,64},{64,56},{72,... | collective-permute-start | bytes 786440 | tf_op jit(solution)/shard_map/ppermute | solution.py:30
  16.3 0.1 collective-permute-start.4
  16.4 0.5 tables.1
  17.0 4.3 %core.1.refs_3_ = f32[2,6,1024,128]{3,2,1,0:T(8,128)S(1)} custom-call(s32[1,1,3,2,4]{4,3,2,1,0:T(2,128)S(1)} %bitcast.7, s32[1,1,3]{2,1,0:T(1,128)S(1)} %copy-done.6, f32[2,6,1024,128]{3,2,1,0:T(8,128)S(1)} %get-tuple-element.43.refs_2_.obj_in, f32[2,6,1024,128]{3,2,1,0:T(8,128)S(1)} %get-tuple-element.37.refs_3_, ...), custom_call_target="tpu_custom_call", output_to_operand_aliasing={{}: (3, {})} | custom-call | flops 2147483648 | bytes 8388608 | tf_op jit(solution)/shard_map/core/pallas_call | solution.py:501
  21.3 0.0 collective-permute-done.1.zb_ref
  21.3 0.8 %sides.1 = (f32[2,6,1024,128]{3,2,1,0:T(8,128)S(1)}, bf16[560,128]{1,0:T(8,128)(2,1)S(1)}, bf16[560,128]{1,0:T(8,128)(2,1)S(1)}, bf16[48,128]{1,0:T(8,128)(2,1)S(1)}) custom-call(s32[1,1,3,2,4]{4,3,2,1,0:T(2,128)S(1)} %bitcast.8, s32[1,1,3]{2,1,0:T(1,128)S(1)} %copy-done.6, ...), custom_call_target="tpu_custom_call", output_to_operand_aliasing={{0}: (2, {})} | custom-call | tf_op jit(solution)/shard_map/sides/pallas_call | solution.py:522
  22.1 3.6 %collective-permute-start.3 = (bf16[560,128]{1,0:T(8,128)(2,1)S(1)}, bf16[560,128]{1,0:T(8,128)(2,1)S(1)}, u32[]{:S(2)}, u32[]{:S(2)}) collective-permute-start(bf16[560,128]{1,0:T(8,128)(2,1)S(1)} %get-tuple-element.49), channel_id=1, source_target_pairs={{8,16},{16,8},{24,32},{32,24},{40,48},{48,40},{56,64},{64,56},{72,... | collective-permute-start | bytes 430088 | tf_op jit(solution)/shard_map/ppermute | solution.py:30
  25.7 0.1 collective-permute-start.5
  25.8 2.5 %inner.1.refs_3_ = f32[2,6,1024,128]{3,2,1,0:T(8,128)S(1)} custom-call(s32[1,1,3,2,4]{4,3,2,1,0:T(2,128)S(1)} %bitcast.9, s32[1,1,3]{2,1,0:T(1,128)S(1)} %copy-done.6, f32[2,6,1024,128]{3,2,1,0:T(8,128)S(1)} %get-tuple-element.46.refs_2_, f32[2,6,1024,128]{3,2,1,0:T(8,128)S(1)} %core.1.refs_3_, ...), custom_call_target="tpu_custom_call", output_to_operand_aliasing={{}: (3, {})} | custom-call | flops 2147483648 | bytes 8388608 | tf_op jit(solution)/shard_map/inner/pallas_call | solution.py:501
  28.3 0.0 collective-permute-done.2.refs_4_
  28.3 2.3 %collective-permute-done.3.refs_5_.yb_ref = bf16[560,128]{1,0:T(8,128)(2,1)S(1)} collective-permute-done((bf16[560,128]{1,0:T(8,128)(2,1)S(1)}, bf16[560,128]{1,0:T(8,128)(2,1)S(1)}, u32[]{:S(2)}, u32[]{:S(2)}) %collective-permute-start.3) | collective-permute-done | bytes 143392 | tf_op jit(solution)/shard_map/ppermute | solution.py:30
  30.6 2.4 %far.1 = (f32[2,6,1024,128]{3,2,1,0:T(8,128)S(1)}, f32[2,6,1024,128]{3,2,1,0:T(8,128)S(1)}, bf16[1664,128]{1,0:T(8,128)(2,1)S(1)}) custom-call(s32[1,1,3,2,4]{4,3,2,1,0:T(2,128)S(1)} %bitcast.10, s32[1,1,3]{2,1,0:T(1,128)S(1)} %copy-done.6, f32[2,6,1024,128]{3,2,1,0:T(8,128)S(1)} %get-tuple-element.46.refs_2_, ...), custom_call_target="tpu_custom_call", output_to_operand_aliasing={{0}: (2, {}), {1}: (3, {})} | custom-call | flops 2147483648 | bytes 8388608 | tf_op jit(solution)/shard_map/far/pallas_call | solution.py:501
  33.0 3.6 %collective-permute-start.7 = (bf16[1664,128]{1,0:T(8,128)(2,1)S(1)}, bf16[1664,128]{1,0:T(8,128)(2,1)S(1)}, u32[]{:S(2)}, u32[]{:S(2)}) collective-permute-start(bf16[1664,128]{1,0:T(8,128)(2,1)S(1)} %get-tuple-element.58), channel_id=1, source_target_pairs={{8,16},{16,8},{24,32},{32,24},{40,48},{48,40},{56,64},{64,56},{72,... | collective-permute-start | bytes 1277960 | tf_op jit(solution)/shard_map/ppermute | solution.py:30
  36.6 2.9 %near.1 = (f32[2,6,1024,128]{3,2,1,0:T(8,128)S(1)}, f32[2,6,1024,128]{3,2,1,0:T(8,128)S(1)}, bf16[1536,128]{1,0:T(8,128)(2,1)S(1)}) custom-call(s32[1,1,3,2,4]{4,3,2,1,0:T(2,128)S(1)} %bitcast.11, s32[1,1,3]{2,1,0:T(1,128)S(1)} %copy-done.6, f32[2,6,1024,128]{3,2,1,0:T(8,128)S(1)} %get-tuple-element.50.refs_2_, ...), custom_call_target="tpu_custom_call", output_to_operand_aliasing={{0}: (2, {}), {1}: (3, {})} | custom-call | flops 2147483648 | bytes 8388608 | tf_op jit(solution)/shard_map/near/pallas_call | solution.py:501
  39.5 0.0 copy-start.1
  39.5 0.1 collective-permute-start.6
  39.6 5.2 %light.1.refs_4_ = f32[4,768,128]{2,1,0:T(8,128)S(1)} custom-call(bf16[48,128]{1,0:T(8,128)(2,1)S(1)} %get-tuple-element.55.meta_ref, bf16[560,128]{1,0:T(8,128)(2,1)S(1)} %collective-permute-done.5.refs_5_.ya_ref, bf16[560,128]{1,0:T(8,128)(2,1)S(1)} %collective-permute-done.3.refs_5_.yb_ref, f32[2,256,256]{2,1,0:T(8,128)S(1)} %copy-done.3), custom_call_target="tpu_custom_call" | custom-call | flops 8388608 | bytes 12582912 | tf_op jit(solution)/shard_map/light/pallas_call | solution.py:537
  44.8 0.2 strips.1
  44.9 0.1 collective-permute-start.9
  45.0 5.6 %collective-permute-start.8 = (bf16[1536,128]{1,0:T(8,128)(2,1)S(1)}, bf16[1536,128]{1,0:T(8,128)(2,1)S(1)}, u32[]{:S(2)}, u32[]{:S(2)}) collective-permute-start(bf16[1536,128]{1,0:T(8,128)(2,1)S(1)} %get-tuple-element.60), channel_id=1, source_target_pairs={{1,2},{2,1},{3,4},{4,3},{5,6},{6,5},{9,10},{10,9},{11,12},{12,11},... | collective-permute-start | bytes 1179656 | tf_op jit(solution)/shard_map/ppermute | solution.py:30
  50.7 1.8 %middle.1 = (f32[2,768,512]{2,1,0:T(8,128)}, f32[2,768,512]{2,1,0:T(8,128)}) custom-call(f32[2,768,512]{2,1,0:T(8,128)S(1)} %copy-done.1, f32[2,6,1024,128]{3,2,1,0:T(8,128)S(1)} %get-tuple-element.56.canvas_ref.refs_1_, bf16[1536,128]{1,0:T(8,128)(2,1)S(1)} %collective-permute-done.6.ya_ref.refs_2_, ...), custom_call_target="tpu_custom_call" | custom-call | flops 4194304 | bytes 10485760 | tf_op jit(solution)/shard_map/middle/pallas_call | solution.py:568
  52.5 3.2 %collective-permute-done.9.refs_5_ = bf16[1536,128]{1,0:T(8,128)(2,1)S(1)} collective-permute-done((bf16[1536,128]{1,0:T(8,128)(2,1)S(1)}, bf16[1536,128]{1,0:T(8,128)(2,1)S(1)}, u32[]{:S(2)}, u32[]{:S(2)}) %collective-permute-start.9) | collective-permute-done | bytes 393248 | tf_op jit(solution)/shard_map/ppermute | solution.py:30
  55.8 1.3 %rim.2 = (f32[2,768,512]{2,1,0:T(8,128)}, f32[2,768,512]{2,1,0:T(8,128)}) custom-call(f32[2,768,512]{2,1,0:T(8,128)S(1)} %copy-done.1, f32[2,6,1024,128]{3,2,1,0:T(8,128)S(1)} %get-tuple-element.56.canvas_ref.refs_1_, bf16[1536,128]{1,0:T(8,128)(2,1)S(1)} %collective-permute-done.6.ya_ref.refs_2_, ...), custom_call_target="tpu_custom_call", output_to_operand_aliasing={{0}: (6, {}), {1}: (7, {})} | custom-call | flops 4194304 | bytes 10485760 | tf_op jit(solution)/shard_map/rim/pallas_call | solution.py:568
  57.0 3.3 %collective-permute-done.8.refs_5_ = bf16[1536,128]{1,0:T(8,128)(2,1)S(1)} collective-permute-done((bf16[1536,128]{1,0:T(8,128)(2,1)S(1)}, bf16[1536,128]{1,0:T(8,128)(2,1)S(1)}, u32[]{:S(2)}, u32[]{:S(2)}) %collective-permute-start.8) | collective-permute-done | bytes 393248 | tf_op jit(solution)/shard_map/ppermute | solution.py:30
  60.4 1.3 %rim.3 = (f32[2,768,512]{2,1,0:T(8,128)}, f32[2,768,512]{2,1,0:T(8,128)}) custom-call(f32[2,768,512]{2,1,0:T(8,128)S(1)} %copy-done.1, f32[2,6,1024,128]{3,2,1,0:T(8,128)S(1)} %get-tuple-element.56.canvas_ref.refs_1_, bf16[1536,128]{1,0:T(8,128)(2,1)S(1)} %collective-permute-done.6.ya_ref.refs_2_, ...), custom_call_target="tpu_custom_call", output_to_operand_aliasing={{0}: (6, {}), {1}: (7, {})} | custom-call | flops 4194304 | bytes 10485760 | tf_op jit(solution)/shard_map/rim/pallas_call | solution.py:568
  (15 shorter events, 0.0 us)
Async XLA Ops:
  0.6 15.8 %copy-start.4 = (bf16[2,256,256]{2,1,0:T(8,128)(2,1)S(1)}, bf16[2,256,256]{2,1,0:T(8,128)(2,1)}, u32[]{:S(2)}) copy-start(bf16[2,256,256]{2,1,0:T(8,128)(2,1)} %constant.2.clone.base_ref) | copy-start | bytes 786436
  0.6 16.3 %copy-start.6 = (s32[1,1,3]{2,1,0:T(1,128)S(1)}, s32[1,1,3]{2,1,0:T(1,128)}, u32[]{:S(2)}) copy-start(s32[1,1,3]{2,1,0:T(1,128)} %refs_1_.7) | copy-start | bytes 40
  0.7 16.3 %copy-start.5 = (s32[1,1,3,4,2]{3,4,2,1,0:T(2,128)S(1)}, s32[1,1,3,4,2]{3,4,2,1,0:T(2,128)}, u32[]{:S(2)}) copy-start(s32[1,1,3,4,2]{3,4,2,1,0:T(2,128)} %param.9) | copy-start | bytes 292
  0.7 16.3 %copy-start.3 = (f32[2,256,256]{2,1,0:T(8,128)S(1)}, f32[2,256,256]{2,1,0:T(8,128)}, u32[]{:S(2)}) copy-start(f32[2,256,256]{2,1,0:T(8,128)} %probe_ref.1) | copy-start | bytes 1572868
  0.7 16.3 %copy-start.2 = (bf16[1,1,3,4,256,256]{5,4,3,2,1,0:T(8,128)(2,1)S(1)}, bf16[1,1,3,4,256,256]{5,4,3,2,1,0:T(8,128)(2,1)}, u32[]{:S(2)}) copy-start(bf16[1,1,3,4,256,256]{5,4,3,2,1,0:T(8,128)(2,1)} %param.8) | copy-start | bytes 4718596
  4.0 17.3 %collective-permute-start = (bf16[1552,128]{1,0:T(8,128)(2,1)}, bf16[1552,128]{1,0:T(8,128)(2,1)S(1)}, u32[]{:S(2)}, u32[]{:S(2)}) collective-permute-start(bf16[1552,128]{1,0:T(8,128)(2,1)} %get-tuple-element.41), channel_id=1, source_target_pairs={{0,1},{1,0},{2,3},{3,2},{4,5},{5,4},{6,7},{7,6},{8,9},{9,8},{10,11... | collective-permute-start | bytes 1191944 | tf_op jit(solution)/shard_map/ppermute | solution.py:30
  4.2 17.1 %collective-permute-start.1 = (bf16[1552,128]{1,0:T(8,128)(2,1)}, bf16[1552,128]{1,0:T(8,128)(2,1)S(1)}, u32[]{:S(2)}, u32[]{:S(2)}) collective-permute-start(bf16[1552,128]{1,0:T(8,128)(2,1)} %get-tuple-element.42), channel_id=1, source_target_pairs={{1,2},{2,1},{3,4},{4,3},{5,6},{6,5},{9,10},{10,9},{11,12},{12,11},... | collective-permute-start | bytes 1191944 | tf_op jit(solution)/shard_map/ppermute | solution.py:30
  9.8 1.9 %copy-start = (f32[2,768,512]{2,1,0:T(8,128)S(1)}, f32[2,768,512]{2,1,0:T(8,128)}, u32[]{:S(2)}) copy-start(f32[2,768,512]{2,1,0:T(8,128)} %refs_0_.5) | copy-start | bytes 9437188
  12.5 15.8 %collective-permute-start.2 = (bf16[1024,128]{1,0:T(8,128)(2,1)S(1)}, bf16[1024,128]{1,0:T(8,128)(2,1)S(1)}, u32[]{:S(2)}, u32[]{:S(2)}) collective-permute-start(bf16[1024,128]{1,0:T(8,128)(2,1)S(1)} %get-tuple-element.48), channel_id=1, source_target_pairs={{8,16},{16,8},{24,32},{32,24},{40,48},{48,40},{56,64},{64,56},{72,... | collective-permute-start | bytes 786440 | tf_op jit(solution)/shard_map/ppermute | solution.py:30
  16.3 20.3 %collective-permute-start.4 = (bf16[1024,128]{1,0:T(8,128)(2,1)S(1)}, bf16[1024,128]{1,0:T(8,128)(2,1)S(1)}, u32[]{:S(2)}, u32[]{:S(2)}) collective-permute-start(bf16[1024,128]{1,0:T(8,128)(2,1)S(1)} %get-tuple-element.52), channel_id=1, source_target_pairs={{0,8},{8,0},{16,24},{24,16},{32,40},{40,32},{48,56},{56,48},{64,72... | collective-permute-start | bytes 786440 | tf_op jit(solution)/shard_map/ppermute | solution.py:30
  22.1 8.5 %collective-permute-start.3 = (bf16[560,128]{1,0:T(8,128)(2,1)S(1)}, bf16[560,128]{1,0:T(8,128)(2,1)S(1)}, u32[]{:S(2)}, u32[]{:S(2)}) collective-permute-start(bf16[560,128]{1,0:T(8,128)(2,1)S(1)} %get-tuple-element.49), channel_id=1, source_target_pairs={{8,16},{16,8},{24,32},{32,24},{40,48},{48,40},{56,64},{64,56},{72,... | collective-permute-start | bytes 430088 | tf_op jit(solution)/shard_map/ppermute | solution.py:30
  25.7 10.9 %collective-permute-start.5 = (bf16[560,128]{1,0:T(8,128)(2,1)S(1)}, bf16[560,128]{1,0:T(8,128)(2,1)S(1)}, u32[]{:S(2)}, u32[]{:S(2)}) collective-permute-start(bf16[560,128]{1,0:T(8,128)(2,1)S(1)} %get-tuple-element.53), channel_id=1, source_target_pairs={{0,8},{8,0},{16,24},{24,16},{32,40},{40,32},{48,56},{56,48},{64,72... | collective-permute-start | bytes 430088 | tf_op jit(solution)/shard_map/ppermute | solution.py:30
  33.0 11.7 %collective-permute-start.7 = (bf16[1664,128]{1,0:T(8,128)(2,1)S(1)}, bf16[1664,128]{1,0:T(8,128)(2,1)S(1)}, u32[]{:S(2)}, u32[]{:S(2)}) collective-permute-start(bf16[1664,128]{1,0:T(8,128)(2,1)S(1)} %get-tuple-element.58), channel_id=1, source_target_pairs={{8,16},{16,8},{24,32},{32,24},{40,48},{48,40},{56,64},{64,56},{72,... | collective-permute-start | bytes 1277960 | tf_op jit(solution)/shard_map/ppermute | solution.py:30
  39.5 11.2 %copy-start.1 = (f32[2,768,512]{2,1,0:T(8,128)S(1)}, f32[2,768,512]{2,1,0:T(8,128)}, u32[]{:S(2)}) copy-start(f32[2,768,512]{2,1,0:T(8,128)} %refs_0_.5) | copy-start | bytes 9437188
  39.5 5.3 %collective-permute-start.6 = (bf16[1536,128]{1,0:T(8,128)(2,1)S(1)}, bf16[1536,128]{1,0:T(8,128)(2,1)S(1)}, u32[]{:S(2)}, u32[]{:S(2)}) collective-permute-start(bf16[1536,128]{1,0:T(8,128)(2,1)S(1)} %get-tuple-element.57), channel_id=1, source_target_pairs={{0,8},{8,0},{16,24},{24,16},{32,40},{40,32},{48,56},{56,48},{64,72... | collective-permute-start | bytes 1179656 | tf_op jit(solution)/shard_map/ppermute | solution.py:30
  44.9 10.8 %collective-permute-start.9 = (bf16[1536,128]{1,0:T(8,128)(2,1)S(1)}, bf16[1536,128]{1,0:T(8,128)(2,1)S(1)}, u32[]{:S(2)}, u32[]{:S(2)}) collective-permute-start(bf16[1536,128]{1,0:T(8,128)(2,1)S(1)} %get-tuple-element.61), channel_id=1, source_target_pairs={{0,1},{1,0},{2,3},{3,2},{4,5},{5,4},{6,7},{7,6},{8,9},{9,8},{10,11... | collective-permute-start | bytes 1179656 | tf_op jit(solution)/shard_map/ppermute | solution.py:30
  45.0 15.3 %collective-permute-start.8 = (bf16[1536,128]{1,0:T(8,128)(2,1)S(1)}, bf16[1536,128]{1,0:T(8,128)(2,1)S(1)}, u32[]{:S(2)}, u32[]{:S(2)}) collective-permute-start(bf16[1536,128]{1,0:T(8,128)(2,1)S(1)} %get-tuple-element.60), channel_id=1, source_target_pairs={{1,2},{2,1},{3,4},{4,3},{5,6},{6,5},{9,10},{10,9},{11,12},{12,11},... | collective-permute-start | bytes 1179656 | tf_op jit(solution)/shard_map/ppermute | solution.py:30
